TPU v7x, 32 devices: a whole 2x2x4 slice. The times are simulated.
32 devices in a mesh: depth: 4 (over z), height: 8 (over y, x, core).
Axes of the slice: x: 2, y: 2, z: 4, core: 2. Of those that a mesh axis runs over, the one named last changes fastest.
Arguments:
- density: float32 [32, 512, 128], P('depth', 'height'), may hold values from -6 to 6
- light_vector: float32 [3], replicated, may hold values from -1 to 1
- colour_gain: float32 [3], replicated, may hold values from 0.5 to 3
- colour_bias: float32 [3], replicated, may hold values from -1 to 1
- shear_step: int32 [4], replicated, may hold values from 0 to 32
- reverse_view: int32 [4], replicated, may hold values from 0 to 1
Outputs:
- images: float32 [4, 4, 512, 128], P(None, None, ('height', 'depth'))
All inputs are finite; a program needn't handle non-finite values.
Results may differ from a plain program's by a relative error of at most 0.0003.
Values sent between devices are 32-bit elements; how exact they have to be, the bound alone decides.
A program may use at most 64 MiB of HBM per device.

v0:
```python
import jax
import jax.numpy as jnp
from jax import lax
from jax.sharding import PartitionSpec as P

EXTINCTION = 2.5


def with_halo(value, sides, width):
    for axis, dim in sides:
        peers, length = (lax.axis_size(axis), value.shape[dim])
        up = [(i, (i + 1) % peers) for i in range(peers - 1)]
        down = [(j, i) for i, j in up]
        last = lax.slice_in_dim(value, length - width, length, axis=dim)
        first = lax.slice_in_dim(value, 0, width, axis=dim)
        before = lax.ppermute(last, axis, up)
        after = lax.ppermute(first, axis, down)
        value = jnp.concatenate([before, value, after], axis=dim)
    return value


def from_partner(block, axis, distance):
    count = lax.axis_size(axis)
    route = []
    for low in range(count):
        high = low | 1 << distance
        if high != low and high < count:
            route += [(low, high), (high, low)]
    return lax.ppermute(block, axis, route)


def shade_block(padded, light_vector, colour_gain, colour_bias, extinction):
    centre = padded[1:-1, 1:-1, 1:-1]
    tilt_depth = 0.5 * (padded[2:, 1:-1, 1:-1] - padded[:-2, 1:-1, 1:-1])
    tilt_rows = 0.5 * (padded[1:-1, 2:, 1:-1] - padded[1:-1, :-2, 1:-1])
    tilt_cols = 0.5 * (padded[1:-1, 1:-1, 2:] - padded[1:-1, 1:-1, :-2])
    facing = (
        light_vector[0] * tilt_depth + light_vector[1] * tilt_rows + light_vector[2] * tilt_cols
    ) * lax.rsqrt(1.0 + tilt_depth * tilt_depth + tilt_rows * tilt_rows + tilt_cols * tilt_cols)
    shading = 0.25 + 1.5 * jnp.maximum(facing, 0.0)
    optical = extinction * jax.nn.softplus(centre)
    opacity = -jnp.expm1(-optical)
    colour = jax.nn.sigmoid(
        colour_gain[:, None, None, None] * centre[None] + colour_bias[:, None, None, None]
    )
    emitted = (opacity * shading)[None] * colour
    return jnp.concatenate([emitted, optical[None]], 0)


def over_front(front, behind):
    return jnp.concatenate(
        [front[:3] + jnp.exp(-front[3:4]) * behind[:3], front[3:4] + behind[3:4]], 0
    )


def on_device(density, light_vector, colour_gain, colour_bias, shear_step, reverse_view):
    planes, rows, cols = density.shape
    groups = lax.axis_size("depth")
    total_planes = planes * groups
    extinction = EXTINCTION / total_planes
    margin_rows = rows // 2
    views = shear_step.shape[0]
    deeper = with_halo(density, (("depth", 0),), 1)
    taller = with_halo(deeper, (("height", 1),), margin_rows + 1)
    taller = jnp.pad(taller[:, margin_rows:, :], ((0, 0), (0, 0), (1, 1)))
    fields = shade_block(taller, light_vector, colour_gain, colour_bias, extinction)
    global_row = lax.axis_index("height") * rows + jnp.arange(rows + margin_rows, dtype=jnp.int32)
    inside = global_row < rows * lax.axis_size("height")
    extended = jnp.where(inside[None, None, :, None], fields, 0.0)
    extra = rows // (2 * groups) + 1
    extended = jnp.pad(extended, ((0, 0), (0, 0), (0, extra), (0, 0)))
    first_plane = lax.axis_index("depth") * planes
    plane_index = jnp.arange(planes, dtype=jnp.int32)

    def view_partial(view):
        step = shear_step[view]
        backward = reverse_view[view]
        base = first_plane * step // total_planes
        zero = jnp.zeros((), jnp.int32)
        window = lax.dynamic_slice(
            extended, (zero, zero, base, zero), (4, planes, rows + extra, cols)
        )
        relative = (first_plane + plane_index) * step // total_planes - base
        sample = jnp.zeros((4, planes, rows, cols), jnp.float32)
        for shift_rows in range(extra + 1):
            picked = (relative == shift_rows)[None, :, None, None]
            sample = jnp.where(picked, window[:, :, shift_rows : shift_rows + rows, :], sample)
        optical = sample[3]
        running = jnp.cumsum(optical, 0)
        depth_sum = running[-1]
        before = jnp.where(backward == 1, depth_sum[None] - running, running - optical)
        colour_sum = jnp.sum(sample[:3] * jnp.exp(-before)[None], 1)
        return jnp.concatenate([colour_sum, depth_sum[None]], 0)

    partial_image = jnp.stack([view_partial(view) for view in range(views)], 1)
    share = rows // groups
    blocks = partial_image.reshape(4, views, groups, share * cols)
    device = lax.axis_index("depth")
    current = blocks
    for level in range(groups.bit_length() - 1):
        count = current.shape[2]
        paired = current.reshape(4, views, count // 2, 2, share * cols)
        digit = device // 2**level % 2
        kept = lax.dynamic_index_in_dim(paired, digit, 3, keepdims=False)
        given = lax.dynamic_index_in_dim(paired, 1 - digit, 3, keepdims=False)
        partner = from_partner(given, "depth", level)
        mine_front = (reverse_view == digit)[None, :, None, None]
        front = jnp.where(mine_front, kept, partner)
        behind = jnp.where(mine_front, partner, kept)
        current = over_front(front, behind)
    final = current[:, :, 0]
    final = final.reshape(4, views, share, cols)
    return jnp.concatenate([final[:3], -jnp.expm1(-final[3:4])], 0)


def solution(mesh):
    placed = (P("depth", "height", None), P(), P(), P(), P(), P())
    return jax.shard_map(
        on_device,
        mesh=mesh,
        in_specs=placed,
        out_specs=P(None, None, ("height", "depth"), None),
        check_vma=False,
    )
```

profile of v0, /device:TPU:2, one launch (start us, length us, event | category | flops | bytes accessed | tf_op | source)
XLA Modules:
  0.0 61.3 jit_solution(12975545454401359276)
XLA Ops:
  0.0 0.8 %fusion.95 = (f32[1,64,128]{2,1,0:T(8,128)S(1)}, f32[1,64,128]{2,1,0:T(8,128)S(1)}) fusion(f32[8,64,128]{2,1,0:T(8,128)} %param.6), kind=kLoop, calls=%fused_computation.251 | loop fusion | bytes 131072 | tf_op jit(solution)/shard_map/slice | solution.py:15
  0.8 3.5 %collective-permute-start = (f32[1,64,128]{2,1,0:T(8,128)S(1)}, f32[1,64,128]{2,1,0:T(8,128)S(1)}, u32[]{:S(2)}, u32[]{:S(2)}) collective-permute-start(f32[1,64,128]{2,1,0:T(8,128)S(1)} %get-tuple-element.34), channel_id=1, source_target_pairs={{0,8},{8,16},{16,24},{1,9},{9,17},{17,25},{2,10},{10,18},{18,26},{... | collective-permute-start | bytes 98312 | tf_op jit(solution)/shard_map/ppermute | solution.py:16
  4.3 1.3 %collective-permute-start.1 = (f32[1,64,128]{2,1,0:T(8,128)S(1)}, f32[1,64,128]{2,1,0:T(8,128)S(1)}, u32[]{:S(2)}, u32[]{:S(2)}) collective-permute-start(f32[1,64,128]{2,1,0:T(8,128)S(1)} %get-tuple-element.33), channel_id=1, source_target_pairs={{8,0},{16,8},{24,16},{9,1},{17,9},{25,17},{10,2},{18,10},{26,18},{... | collective-permute-start | bytes 98312 | tf_op jit(solution)/shard_map/ppermute | solution.py:17
  5.6 1.4 %fusion.97 = (s32[1]{0:T(128)}, s32[1]{0:T(128)}, s32[1]{0:T(128)}, s32[1]{0:T(128)}) fusion(s32[4]{0:T(128)} %param.10), kind=kLoop, calls=%fused_computation.253 | loop fusion | bytes 32 | tf_op jit(solution)/shard_map/slice | solution.py:76
  9.5 1.2 %broadcast_compare_fusion.24 = (pred[8]{0:T(512)(128)(4,1)S(1)}, s32[8]{0:T(128)S(1)}, pred[8]{0:T(512)(128)(4,1)S(1)}, s32[8]{0:T(128)S(1)}) fusion(s32[]{:T(128)S(6)} %select_n.416, s32[]{:T(128)} %bitcast.22, s32[]{:T(128)S(6)} %mul.313, s32[]{:T(128)S(6)} %select_n.401, s32[]{:T(128)} %bitcast.16), kind=kLoop, calls=%fused_computation.228 | loop fusion | flops 296 | bytes 100 | tf_op jit(solution)/shard_map/eq | solution.py:86
  10.8 1.4 %fusion.98 = (f32[1]{0:T(128)}, f32[1]{0:T(128)}, f32[1]{0:T(128)}) fusion(f32[3]{0:T(128)} %param.7), kind=kLoop, calls=%fused_computation.254 | loop fusion | bytes 24 | tf_op jit(solution)/shard_map/slice | solution.py:38
  12.2 1.5 %fusion.96 = (s32[1]{0:T(128)}, s32[1]{0:T(128)}, s32[1]{0:T(128)}, s32[1]{0:T(128)}) fusion(s32[4]{0:T(128)} %param.11), kind=kLoop, calls=%fused_computation.252 | loop fusion | bytes 32 | tf_op jit(solution)/shard_map/slice | solution.py:77
  13.7 1.3 %broadcast_compare_fusion.26 = (pred[8]{0:T(512)(128)(4,1)S(1)}, s32[8]{0:T(128)S(1)}, pred[8]{0:T(512)(128)(4,1)S(1)}, s32[8]{0:T(128)S(1)}) fusion(s32[]{:T(128)S(6)} %select_n.386, s32[]{:T(128)} %bitcast.10, s32[]{:T(128)S(6)} %mul.313, s32[]{:T(128)S(6)} %select_n.369, s32[]{:T(128)} %bitcast), kind=kLoop, calls=%fused_computation.230 | loop fusion | flops 296 | bytes 100 | tf_op jit(solution)/shard_map/eq | solution.py:86
  19.4 0.0 collective-permute-done
  19.4 1.0 %constant_dynamic-update-slice_fusion.1 = f32[10,64,128]{2,1,0:T(8,128)S(1)} fusion(f32[10,64,128]{2,1,0:T(8,128)S(1)} %constant_dynamic-update-slice_fusion.2, f32[8,64,128]{2,1,0:T(8,128)} %param.6), kind=kLoop, calls=%fused_computation.174 | loop fusion | bytes 524288
  20.4 0.0 collective-permute-done.1
  20.4 1.9 %collective-permute-start.2 = (f32[10,33,128]{2,1,0:T(8,128)S(1)}, f32[10,33,128]{2,1,0:T(8,128)S(1)}, u32[]{:S(2)}, u32[]{:S(2)}) collective-permute-start(f32[10,33,128]{2,1,0:T(8,128)S(1)} %get-tuple-element.22), channel_id=1, source_target_pairs={{1,0},{2,1},{3,2},{4,3},{5,4},{6,5},{7,6},{9,8},{10,9},{11,10},{12... | collective-permute-start | bytes 506888 | tf_op jit(solution)/shard_map/ppermute | solution.py:17
  22.4 2.4 %collective-permute-start.3 = (f32[10,33,128]{2,1,0:T(8,128)S(1)}, f32[10,33,128]{2,1,0:T(8,128)S(1)}, u32[]{:S(2)}, u32[]{:S(2)}) collective-permute-start(f32[10,33,128]{2,1,0:T(8,128)S(1)} %get-tuple-element.21), channel_id=1, source_target_pairs={{0,1},{1,2},{2,3},{3,4},{4,5},{5,6},{6,7},{8,9},{9,10},{10,11},{11... | collective-permute-start | bytes 506888 | tf_op jit(solution)/shard_map/ppermute | solution.py:16
  24.8 0.8 %collective-permute-done.2 = f32[10,33,128]{2,1,0:T(8,128)S(1)} collective-permute-done((f32[10,33,128]{2,1,0:T(8,128)S(1)}, f32[10,33,128]{2,1,0:T(8,128)S(1)}, u32[]{:S(2)}, u32[]{:S(2)}) %collective-permute-start.2) | collective-permute-done | bytes 168992 | tf_op jit(solution)/shard_map/ppermute | solution.py:17
  25.6 3.8 %collective-permute-done.3 = f32[10,33,128]{2,1,0:T(8,128)S(1)} collective-permute-done((f32[10,33,128]{2,1,0:T(8,128)S(1)}, f32[10,33,128]{2,1,0:T(8,128)S(1)}, u32[]{:S(2)}, u32[]{:S(2)}) %collective-permute-start.3) | collective-permute-done | bytes 168992 | tf_op jit(solution)/shard_map/ppermute | solution.py:16
  29.4 0.1 pad_maximum_fusion
  29.5 0.0 copy-start.1
  29.6 0.0 copy-start.2
  29.6 0.9 %add_multiply_fusion = (f32[8,96,128]{2,1,0:T(8,128)S(1)}, f32[8,96,128]{2,1,0:T(8,128)S(1)}) fusion(f32[10,98,128]{2,1,0:T(8,128)S(1)} %slice.364, f32[10,130,128]{2,1,0:T(8,128)S(1)} %pad_maximum_fusion, f32[10,33,128]{2,1,0:T(8,128)S(1)} %collective-permute-done.2, f32[10,64,128]{2,1,0:T(8,128)S(1)} %constant_dynamic-update-slice_fusion, f32[]{:T(128)} %bitcast.3, ...), kind=kLoop, calls=%fused_computation.108 | loop fusion | flops 3440640 | bytes 2178060 | tf_op jit(solution)/shard_map/mul | solution.py:46
  30.4 0.2 fusion.79
  30.7 0.0 copy-done.1
  30.7 0.0 copy-done.2
  30.7 0.4 divide_multiply_fusion
  31.1 0.3 maximum_select_fusion
  31.4 2.2 %fusion.39 = f32[4,8,64,128]{3,2,1,0:T(8,128)S(1)} fusion(s32[]{:T(128)S(6)} %select_n.417, f32[4,8,96,128]{3,2,1,0:T(8,128)S(1)} %maximum_select_fusion, s32[]{:T(128)S(6)} %add.424, s32[]{:T(128)S(6)} %add.425, s32[]{:T(128)S(6)} %add.426, s32[]{:T(128)S(6)} %add.427, s32[]{:T(128)S(6)} %add.428, s32[]{:T(128)S(6)} %add.429, s32[]{:T(128)S(6)} %add.430, ...), kind=kLoop, calls=%fused_computation.84 | loop fusion | flops 2621440 | bytes 2621560 | tf_op jit(solution)/shard_map/jit(_where)/select_n | solution.py:87
  33.7 0.1 fusion.53
  33.7 0.1 fusion.40
  33.8 0.1 stack.18
  33.9 2.2 %fusion.29 = f32[4,8,64,128]{3,2,1,0:T(8,128)S(1)} fusion(s32[]{:T(128)S(6)} %select_n.402, f32[4,8,96,128]{3,2,1,0:T(8,128)S(1)} %maximum_select_fusion, s32[]{:T(128)S(6)} %add.415, s32[]{:T(128)S(6)} %add.416, s32[]{:T(128)S(6)} %add.417, s32[]{:T(128)S(6)} %add.418, s32[]{:T(128)S(6)} %add.419, s32[]{:T(128)S(6)} %add.420, s32[]{:T(128)S(6)} %add.421, ...), kind=kLoop, calls=%fused_computation.74 | loop fusion | flops 2621440 | bytes 2621560 | tf_op jit(solution)/shard_map/jit(_where)/select_n | solution.py:87
  36.2 0.1 fusion.59
  36.3 0.1 fusion.41
  36.4 0.1 stack.17
  36.4 2.2 %fusion.19 = f32[4,8,64,128]{3,2,1,0:T(8,128)S(1)} fusion(s32[]{:T(128)S(6)} %select_n.387, f32[4,8,96,128]{3,2,1,0:T(8,128)S(1)} %maximum_select_fusion, s32[]{:T(128)S(6)} %add.406, s32[]{:T(128)S(6)} %add.407, s32[]{:T(128)S(6)} %add.408, s32[]{:T(128)S(6)} %add.409, s32[]{:T(128)S(6)} %add.410, s32[]{:T(128)S(6)} %add.411, s32[]{:T(128)S(6)} %add.412, ...), kind=kLoop, calls=%fused_computation.64 | loop fusion | flops 2621440 | bytes 2621560 | tf_op jit(solution)/shard_map/jit(_where)/select_n | solution.py:87
  38.7 0.1 fusion.65
  38.8 0.1 fusion.42
  38.9 0.1 stack.16
  39.0 2.2 %fusion.9 = f32[4,8,64,128]{3,2,1,0:T(8,128)S(1)} fusion(s32[]{:T(128)S(6)} %select_n.372, f32[4,8,96,128]{3,2,1,0:T(8,128)S(1)} %maximum_select_fusion, s32[]{:T(128)S(6)} %add.397, s32[]{:T(128)S(6)} %add.398, s32[]{:T(128)S(6)} %add.399, s32[]{:T(128)S(6)} %add.400, s32[]{:T(128)S(6)} %add.401, s32[]{:T(128)S(6)} %add.402, s32[]{:T(128)S(6)} %add.403, ...), kind=kLoop, calls=%fused_computation.54 | loop fusion | flops 2621440 | bytes 2621560 | tf_op jit(solution)/shard_map/jit(_where)/select_n | solution.py:87
  41.3 0.1 fusion.71
  41.4 0.1 fusion.43
  41.5 0.1 stack.15
  41.6 0.0 copy-start
  41.7 0.6 constant_dynamic-slice_fusion.1
  42.2 0.1 copy.18
  42.4 3.0 %collective-permute-start.4 = (f32[4,4,2,2048]{3,2,0,1:T(2,128)S(1)}, f32[4,4,2,2048]{3,2,0,1:T(2,128)S(1)}, u32[]{:S(2)}, u32[]{:S(2)}) collective-permute-start(f32[4,4,2,2048]{3,2,0,1:T(2,128)S(1)} %bitcast.107), channel_id=1, source_target_pairs={{0,8},{8,0},{16,24},{24,16},{1,9},{9,1},{17,25},{25,17},{2,10},{10... | collective-permute-start | bytes 786440 | tf_op jit(solution)/shard_map/ppermute | solution.py:29
  45.3 0.0 copy-done
  45.3 5.9 %collective-permute-done.4 = f32[4,4,2,2048]{3,2,0,1:T(2,128)S(1)} collective-permute-done((f32[4,4,2,2048]{3,2,0,1:T(2,128)S(1)}, f32[4,4,2,2048]{3,2,0,1:T(2,128)S(1)}, u32[]{:S(2)}, u32[]{:S(2)}) %collective-permute-start.4) | collective-permute-done | bytes 262176 | tf_op jit(solution)/shard_map/ppermute | solution.py:29
  51.2 0.3 bitcast_select_fusion.1
  51.6 0.1 slice_add_fusion
  51.6 0.1 fusion.78
  51.8 0.1 fusion.80
  51.9 2.8 %collective-permute-start.5 = (f32[4,4,1,2048]{3,2,0,1:T(1,128)S(1)}, f32[4,4,1,2048]{3,2,0,1:T(1,128)S(1)}, u32[]{:S(2)}, u32[]{:S(2)}) collective-permute-start(f32[4,4,1,2048]{3,2,0,1:T(1,128)S(1)} %fusion.80), channel_id=1, source_target_pairs={{0,16},{16,0},{8,24},{24,8},{1,17},{17,1},{9,25},{25,9},{2,18},{18... | collective-permute-start | bytes 393224 | tf_op jit(solution)/shard_map/ppermute | solution.py:29
  54.8 5.2 %collective-permute-done.5 = f32[4,4,1,2048]{3,2,0,1:T(1,128)S(1)} collective-permute-done((f32[4,4,1,2048]{3,2,0,1:T(1,128)S(1)}, f32[4,4,1,2048]{3,2,0,1:T(1,128)S(1)}, u32[]{:S(2)}, u32[]{:S(2)}) %collective-permute-start.5) | collective-permute-done | bytes 131104 | tf_op jit(solution)/shard_map/ppermute | solution.py:29
  60.0 0.2 broadcast_select_fusion.1
  60.2 0.2 broadcast_select_fusion
  60.4 0.1 negate_exponential_fusion
  60.6 0.1 fusion.82
  60.7 0.7 %pad_maximum_fusion.6 = f32[4,4,16,128]{3,2,1,0:T(8,128)} fusion(f32[1,4,16,128]{3,2,1,0:T(8,128)S(1)} %bitcast.109, f32[3,4,16,128]{3,2,0,1:T(8,128)S(1)} %bitcast.106), kind=kLoop, calls=%fused_computation.163 | loop fusion | flops 32768 | bytes 262144 | tf_op jit(solution)/shard_map/concatenate | solution.py:113
  (27 shorter events, 0.4 us)
Async XLA Ops:
  0.8 18.6 %collective-permute-start = (f32[1,64,128]{2,1,0:T(8,128)S(1)}, f32[1,64,128]{2,1,0:T(8,128)S(1)}, u32[]{:S(2)}, u32[]{:S(2)}) collective-permute-start(f32[1,64,128]{2,1,0:T(8,128)S(1)} %get-tuple-element.34), channel_id=1, source_target_pairs={{0,8},{8,16},{16,24},{1,9},{9,17},{17,25},{2,10},{10,18},{18,26},{... | collective-permute-start | bytes 98312 | tf_op jit(solution)/shard_map/ppermute | solution.py:16
  4.3 16.1 %collective-permute-start.1 = (f32[1,64,128]{2,1,0:T(8,128)S(1)}, f32[1,64,128]{2,1,0:T(8,128)S(1)}, u32[]{:S(2)}, u32[]{:S(2)}) collective-permute-start(f32[1,64,128]{2,1,0:T(8,128)S(1)} %get-tuple-element.33), channel_id=1, source_target_pairs={{8,0},{16,8},{24,16},{9,1},{17,9},{25,17},{10,2},{18,10},{26,18},{... | collective-permute-start | bytes 98312 | tf_op jit(solution)/shard_map/ppermute | solution.py:17
  20.4 5.2 %collective-permute-start.2 = (f32[10,33,128]{2,1,0:T(8,128)S(1)}, f32[10,33,128]{2,1,0:T(8,128)S(1)}, u32[]{:S(2)}, u32[]{:S(2)}) collective-permute-start(f32[10,33,128]{2,1,0:T(8,128)S(1)} %get-tuple-element.22), channel_id=1, source_target_pairs={{1,0},{2,1},{3,2},{4,3},{5,4},{6,5},{7,6},{9,8},{10,9},{11,10},{12... | collective-permute-start | bytes 506888 | tf_op jit(solution)/shard_map/ppermute | solution.py:17
  22.4 7.1 %collective-permute-start.3 = (f32[10,33,128]{2,1,0:T(8,128)S(1)}, f32[10,33,128]{2,1,0:T(8,128)S(1)}, u32[]{:S(2)}, u32[]{:S(2)}) collective-permute-start(f32[10,33,128]{2,1,0:T(8,128)S(1)} %get-tuple-element.21), channel_id=1, source_target_pairs={{0,1},{1,2},{2,3},{3,4},{4,5},{5,6},{6,7},{8,9},{9,10},{10,11},{11... | collective-permute-start | bytes 506888 | tf_op jit(solution)/shard_map/ppermute | solution.py:16
  29.5 1.1 %copy-start.1 = (f32[3]{0:T(128)S(1)}, f32[3]{0:T(128)}, u32[]{:S(2)}) copy-start(f32[3]{0:T(128)} %param.9) | copy-start | bytes 40
  29.6 1.1 %copy-start.2 = (f32[3]{0:T(128)S(1)}, f32[3]{0:T(128)}, u32[]{:S(2)}) copy-start(f32[3]{0:T(128)} %param.8) | copy-start | bytes 40
  41.6 3.8 %copy-start = (s32[4]{0:T(128)S(1)}, s32[4]{0:T(128)}, u32[]{:S(2)}) copy-start(s32[4]{0:T(128)} %param.11) | copy-start | bytes 52
  42.4 8.9 %collective-permute-start.4 = (f32[4,4,2,2048]{3,2,0,1:T(2,128)S(1)}, f32[4,4,2,2048]{3,2,0,1:T(2,128)S(1)}, u32[]{:S(2)}, u32[]{:S(2)}) collective-permute-start(f32[4,4,2,2048]{3,2,0,1:T(2,128)S(1)} %bitcast.107), channel_id=1, source_target_pairs={{0,8},{8,0},{16,24},{24,16},{1,9},{9,1},{17,25},{25,17},{2,10},{10... | collective-permute-start | bytes 786440 | tf_op jit(solution)/shard_map/ppermute | solution.py:29
  51.9 8.0 %collective-permute-start.5 = (f32[4,4,1,2048]{3,2,0,1:T(1,128)S(1)}, f32[4,4,1,2048]{3,2,0,1:T(1,128)S(1)}, u32[]{:S(2)}, u32[]{:S(2)}) collective-permute-start(f32[4,4,1,2048]{3,2,0,1:T(1,128)S(1)} %fusion.80), channel_id=1, source_target_pairs={{0,16},{16,0},{8,24},{24,8},{1,17},{17,1},{9,25},{25,9},{2,18},{18... | collective-permute-start | bytes 393224 | tf_op jit(solution)/shard_map/ppermute | solution.py:29
where the time goes:
time: 61.8 us; the launch traced here: 61.3 us
  other arithmetic  16.1 us (26%)
  waiting for transfers between devices  15.7 us (25%)
  starting transfers between devices  14.9 us (24%)
  between operations  7.48 us (12%)
  local copies, waits for them, and re-layouts  7.21 us (12%)
    ppermute x2, waiting for transfers between devices, from_partner(): return lax.ppermute(block, axis, route)  11.1 us
    select_n x4, other arithmetic, view_partial(): jnp.where(picked, window[:, :, shift_rows:shift_rows + rows, :], sample)  9 us
    ppermute x2, starting transfers between devices, with_halo(): before = lax.ppermute(last, axis, up)  5.88 us
    ppermute x2, starting transfers between devices, from_partner(): return lax.ppermute(block, axis, route)  5.81 us
    ppermute x2, waiting for transfers between devices, with_halo(): before = lax.ppermute(last, axis, up)  3.82 us
    ppermute x2, starting transfers between devices, with_halo(): after = lax.ppermute(first, axis, down)  3.21 us
    eq x6, other arithmetic, view_partial(): picked = (relative == shift_rows)[None, :, None, None]  2.53 us
    slice x1, local copies, waits for them, and re-layouts, view_partial(): backward = reverse_view[view]  1.46 us
  transfers between devices with their start and end apart: 6, of which 4 were waited for; matrix products, arithmetic and copies ran while one was open for 13% of the time, Pallas kernels for 0%

commit v1 on v0

v1 whole, which is shorter than its diff:
```python
import functools

import jax
import jax.numpy as jnp
from jax import lax
from jax.experimental import pallas as pl
from jax.experimental.pallas import tpu as pltpu
from jax.sharding import PartitionSpec as P

EXTINCTION = 2.5
LEAD = 8
MESH = pl.DeviceIdType.MESH


def spans(low, high, size):
    return [(at, min(size, high - at)) for at in range(low, high, size)]


def kernel(
    groups,
    towers,
    density,
    light,
    gain,
    bias,
    shear,
    reverse,
    out,
    volume,
    fields,
    outgoing,
    incoming,
    local_sem,
    halo_send,
    halo_recv,
    part_send,
    part_recv,
):
    planes, rows, cols = density.shape
    margin = rows // 2
    views = shear.shape[0]
    share = rows // groups
    total_planes = planes * groups
    extinction = EXTINCTION / total_planes
    d = lax.axis_index("depth")
    h = lax.axis_index("height")
    end = LEAD + rows
    tall = end + margin

    own = pltpu.make_async_copy(
        density, volume.at[pl.ds(1, planes), pl.ds(LEAD, rows)], local_sem
    )
    own.start()

    def near(step_d, step_h):
        ok = None
        for at, step, count in ((d, step_d, groups), (h, step_h, towers)):
            if step:
                test = (at + step >= 0) & (at + step < count)
                ok = test if ok is None else ok & test
        return ok, (d + step_d, h + step_h)

    barrier = pltpu.get_barrier_semaphore()
    beside = [(0, 1), (0, -1), (1, 1), (1, -1), (-1, 1), (-1, -1)]
    expected = jnp.int32(groups - 1)
    for hop in range(1, groups):
        pl.semaphore_signal(
            barrier, inc=1, device_id=(lax.rem(d + hop, groups), h), device_id_type=MESH
        )
    for step_d, step_h in beside:
        ok, target = near(step_d, step_h)
        expected = expected + jnp.where(ok, 1, 0)

        @pl.when(ok)
        def _(target=target):
            pl.semaphore_signal(barrier, inc=1, device_id=target, device_id_type=MESH)

    @pl.when(d == 0)
    def _():
        volume[0] = jnp.zeros(volume.shape[1:], jnp.float32)

    @pl.when(d == groups - 1)
    def _():
        volume[planes + 1] = jnp.zeros(volume.shape[1:], jnp.float32)

    @pl.when(h == 0)
    def _():
        volume[1 : planes + 1, :LEAD] = jnp.zeros((planes, LEAD, cols), jnp.float32)

    @pl.when(h == towers - 1)
    def _():
        volume[:, end:tall] = jnp.zeros((planes + 2, margin, cols), jnp.float32)

    pl.semaphore_wait(barrier, expected)

    whole = pl.ds(0, planes)
    inner = pl.ds(1, planes)
    first, last = pl.ds(0, 1), pl.ds(planes - 1, 1)
    low, high = pl.ds(0, 1), pl.ds(planes + 1, 1)
    routes = [
        ((0, -1), whole, (0, margin), inner, end),
        ((1, -1), last, (0, margin), low, end),
        ((-1, -1), first, (0, margin), high, end),
        ((1, 0), last, (0, rows), low, LEAD),
        ((-1, 0), first, (0, rows), high, LEAD),
        ((0, 1), whole, (rows - LEAD, LEAD), inner, 0),
    ]

    def halo(index, reach):
        step, from_planes, (row, count), to_planes, to_row = routes[index]
        return pltpu.make_async_remote_copy(
            src_ref=density.at[from_planes, pl.ds(row, count)],
            dst_ref=volume.at[to_planes, pl.ds(to_row, count)],
            send_sem=halo_send.at[index],
            recv_sem=halo_recv.at[index],
            device_id=reach,
            device_id_type=MESH,
        )

    for index, route in enumerate(routes):
        ok, target = near(*route[0])

        @pl.when(ok)
        def _(index=index, target=target):
            halo(index, target).start()

    own.wait()

    lz, ly, lx = light[0], light[1], light[2]
    half_gain = [0.5 * gain[c] for c in range(3)]
    half_bias = [0.5 * bias[c] for c in range(3)]

    def shade(plane, row, count, keep):
        at = LEAD + row
        centre = volume[plane, at : at + count]
        lane = lax.broadcasted_iota(jnp.int32, (count, cols), 1)
        following = jnp.where(lane == cols - 1, 0.0, pltpu.roll(centre, cols - 1, 1))
        previous = jnp.where(lane == 0, 0.0, pltpu.roll(centre, 1, 1))
        dx = following - previous
        dz = volume[plane + 1, at : at + count] - volume[plane - 1, at : at + count]
        dy = volume[plane, at + 1 : at + 1 + count] - volume[plane, at - 1 : at - 1 + count]
        facing = (lz * dz + ly * dy + lx * dx) * lax.rsqrt(4.0 + dz * dz + dy * dy + dx * dx)
        shading = 0.25 + 1.5 * jnp.maximum(facing, 0.0)
        optical = extinction * (
            jnp.maximum(centre, 0.0) + jnp.log1p(jnp.exp(-jnp.abs(centre)))
        )
        opacity = jnp.tanh(0.5 * optical) * (1.0 + jnp.exp(-optical))
        if keep is not None:
            opacity = opacity * keep
        lit = 0.5 * (opacity * shading)
        to = pl.ds(row, count)
        for c in range(3):
            fields[c, plane - 1, to] = lit + lit * jnp.tanh(half_gain[c] * centre + half_bias[c])
        fields[3, plane - 1, to] = opacity

    inside = jnp.where(h < towers - 1, 1.0, 0.0)

    def early(plane, _):
        for row, count in spans(LEAD, rows - LEAD, 16):
            shade(plane, row, count, None)
        return 0

    lax.fori_loop(2, planes, early, 0)

    for index, route in enumerate(routes):
        step_d, step_h = route[0]
        ok, source = near(-step_d, -step_h)

        @pl.when(ok)
        def _(index=index, source=source):
            halo(index, source).wait_recv()

    def late(plane, _):
        shade(plane, 0, LEAD, None)
        shade(plane, rows - LEAD, LEAD, None)
        for row, count in spans(rows, rows + margin, 16):
            shade(plane, row, count, inside)
        return 0

    lax.fori_loop(1, planes + 1, late, 0)
    for plane in (1, planes):
        for row, count in spans(LEAD, rows - LEAD, 16):
            shade(plane, row, count, None)

    first_plane = d * planes

    def partial(view, block):
        step = shear[view]
        backward = reverse[view]
        colour = [jnp.zeros((share, cols), jnp.float32) for _ in range(3)]
        clear = jnp.ones((share, cols), jnp.float32)
        covered = jnp.zeros((share, cols), jnp.float32)
        for i in range(planes):
            plane = i + backward * (planes - 1 - 2 * i)
            offset = lax.div((first_plane + plane) * step, jnp.int32(total_planes))
            at = pl.ds(offset + block * share, share)
            for c in range(3):
                colour[c] = colour[c] + clear * fields[c, plane, at]
            covered = covered + clear * fields[3, plane, at]
            clear = 1.0 - covered
        return colour + [covered]

    def send(view, hop):
        peer = lax.rem(d + hop, groups)
        return pltpu.make_async_remote_copy(
            src_ref=outgoing.at[peer, view],
            dst_ref=incoming.at[d, view],
            send_sem=part_send.at[view, hop],
            recv_sem=part_recv.at[view, d],
            device_id=(peer, h),
            device_id_type=MESH,
        )

    for view in range(views):

        def one_peer(hop, _):
            peer = lax.rem(d + hop, groups)
            image = partial(view, peer)
            for c in range(4):
                outgoing[peer, view, c] = image[c]
            send(view, hop).start()
            return 0

        lax.fori_loop(1, groups, one_peer, 0)

    for view in range(views):
        image = partial(view, d)
        for c in range(4):
            incoming[d, view, c] = image[c]

    for view in range(views):

        def arrived(hop, _):
            source = lax.rem(d + hop, groups)
            pltpu.make_async_remote_copy(
                src_ref=outgoing.at[source, view],
                dst_ref=incoming.at[source, view],
                send_sem=part_send.at[view, hop],
                recv_sem=part_recv.at[view, source],
                device_id=(source, h),
                device_id_type=MESH,
            ).wait_recv()
            return 0

        lax.fori_loop(1, groups, arrived, 0)
        swap = reverse[view] == 1
        total = [incoming[0, view, c] for c in range(4)]
        for g in range(1, groups):
            new = [incoming[g, view, c] for c in range(4)]
            front = [jnp.where(swap, b, a) for a, b in zip(total, new)]
            behind = [jnp.where(swap, a, b) for a, b in zip(total, new)]
            clear = 1.0 - front[3]
            total = [f + clear * b for f, b in zip(front, behind)]
        for c in range(4):
            out[c, view] = total[c]

    for index, route in enumerate(routes):
        ok, target = near(*route[0])

        @pl.when(ok)
        def _(index=index, target=target):
            halo(index, target).wait_send()

    for view in range(views):

        def sent(hop, _):
            send(view, hop).wait_send()
            return 0

        lax.fori_loop(1, groups, sent, 0)


def on_device(groups, towers, density, light, gain, bias, shear, reverse):
    planes, rows, cols = density.shape
    views = shear.shape[0]
    share = rows // groups
    tall = LEAD + rows + rows // 2
    scalars = pl.BlockSpec(memory_space=pltpu.SMEM)
    return pl.pallas_call(
        functools.partial(kernel, groups, towers),
        name="render",
        out_shape=jax.ShapeDtypeStruct((4, views, share, cols), jnp.float32),
        in_specs=[pl.BlockSpec(memory_space=pl.ANY)] + [scalars] * 5,
        out_specs=pl.BlockSpec(memory_space=pltpu.VMEM),
        scratch_shapes=[
            pltpu.VMEM((planes + 2, tall + LEAD, cols), jnp.float32),
            pltpu.VMEM((4, planes, rows + rows // 2, cols), jnp.float32),
            pltpu.VMEM((groups, views, 4, share, cols), jnp.float32),
            pltpu.VMEM((groups, views, 4, share, cols), jnp.float32),
            pltpu.SemaphoreType.DMA,
            pltpu.SemaphoreType.DMA((6,)),
            pltpu.SemaphoreType.DMA((6,)),
            pltpu.SemaphoreType.DMA((views, groups)),
            pltpu.SemaphoreType.DMA((views, groups)),
        ],
        compiler_params=pltpu.CompilerParams(collective_id=0, has_side_effects=True),
    )(density, light, gain, bias, shear, reverse)


def solution(mesh):
    groups, towers = mesh.shape["depth"], mesh.shape["height"]
    placed = (P("depth", "height", None), P(), P(), P(), P(), P())
    return jax.shard_map(
        functools.partial(on_device, groups, towers),
        mesh=mesh,
        in_specs=placed,
        out_specs=P(None, None, ("height", "depth"), None),
        check_vma=False,
    )
```

time: 61.8 us -> 25.6 us (0.41)
  the two profiles are of different devices: /device:TPU:2 before, /device:TPU:0 now
where the time goes in v1:
time: 25.6 us; the launch traced here: 25.4 us
  Pallas kernels  23.8 us (93%)
  local copies, waits for them, and re-layouts  1.57 us (6%)
    pallas_call x1, Pallas kernels, on_device(): pl.pallas_call(functools.partial(kernel, groups, towers), name='render',...  23.8 us
    unnamed x1, local copies, waits for them, and re-layouts  1.57 us

profile of v1, /device:TPU:0, one launch (start us, length us, event | category | flops | bytes accessed | tf_op | source)
XLA Modules:
  0.0 25.4 jit_solution(8250637634387074422)
XLA Ops:
  0.0 23.8 %render.1 = f32[4,4,16,128]{3,2,1,0:T(8,128)} custom-call(f32[8,64,128]{2,1,0:T(8,128)} %density.1, f32[3]{0:T(128)} %light.1, f32[3]{0:T(128)} %gain.1, f32[3]{0:T(128)} %bias.1, s32[4]{0:T(128)} %shear.1, s32[4]{0:T(128)} %reverse.1), custom_call_target="tpu_custom_call" | custom-call | tf_op jit(solution)/shard_map/render/pallas_call | solution.py:279
  23.9 1.6 %copy.8 = f32[4,4,16,128]{3,2,1,0:T(8,128)} copy(f32[4,4,16,128]{3,2,1,0:T(8,128)} %render.1) | data formatting | bytes 262144

commit v2 on v1

--- a/solution.py
+++ b/solution.py
@@ -30,9 +30,12 @@
     fields,
     outgoing,
     incoming,
+    handed,
     local_sem,
     halo_send,
     halo_recv,
+    hand_send,
+    hand_recv,
     part_send,
     part_recv,
 ):
@@ -91,39 +94,6 @@
     def _():
         volume[:, end:tall] = jnp.zeros((planes + 2, margin, cols), jnp.float32)
 
-    pl.semaphore_wait(barrier, expected)
-
-    whole = pl.ds(0, planes)
-    inner = pl.ds(1, planes)
-    first, last = pl.ds(0, 1), pl.ds(planes - 1, 1)
-    low, high = pl.ds(0, 1), pl.ds(planes + 1, 1)
-    routes = [
-        ((0, -1), whole, (0, margin), inner, end),
-        ((1, -1), last, (0, margin), low, end),
-        ((-1, -1), first, (0, margin), high, end),
-        ((1, 0), last, (0, rows), low, LEAD),
-        ((-1, 0), first, (0, rows), high, LEAD),
-        ((0, 1), whole, (rows - LEAD, LEAD), inner, 0),
-    ]
-
-    def halo(index, reach):
-        step, from_planes, (row, count), to_planes, to_row = routes[index]
-        return pltpu.make_async_remote_copy(
-            src_ref=density.at[from_planes, pl.ds(row, count)],
-            dst_ref=volume.at[to_planes, pl.ds(to_row, count)],
-            send_sem=halo_send.at[index],
-            recv_sem=halo_recv.at[index],
-            device_id=reach,
-            device_id_type=MESH,
-        )
-
-    for index, route in enumerate(routes):
-        ok, target = near(*route[0])
-
-        @pl.when(ok)
-        def _(index=index, target=target):
-            halo(index, target).start()
-
     own.wait()
 
     lz, ly, lx = light[0], light[1], light[2]
@@ -161,6 +131,39 @@
         return 0
 
     lax.fori_loop(2, planes, early, 0)
+
+    pl.semaphore_wait(barrier, expected)
+
+    whole = pl.ds(0, planes)
+    inner = pl.ds(1, planes)
+    first, last = pl.ds(0, 1), pl.ds(planes - 1, 1)
+    low, high = pl.ds(0, 1), pl.ds(planes + 1, 1)
+    routes = [
+        ((0, -1), whole, (0, margin), inner, end),
+        ((1, -1), last, (0, margin), low, end),
+        ((-1, -1), first, (0, margin), high, end),
+        ((1, 0), last, (0, rows), low, LEAD),
+        ((-1, 0), first, (0, rows), high, LEAD),
+        ((0, 1), whole, (rows - LEAD, LEAD), inner, 0),
+    ]
+
+    def halo(index, reach):
+        step, from_planes, (row, count), to_planes, to_row = routes[index]
+        return pltpu.make_async_remote_copy(
+            src_ref=density.at[from_planes, pl.ds(row, count)],
+            dst_ref=volume.at[to_planes, pl.ds(to_row, count)],
+            send_sem=halo_send.at[index],
+            recv_sem=halo_recv.at[index],
+            device_id=reach,
+            device_id_type=MESH,
+        )
+
+    for index, route in enumerate(routes):
+        ok, target = near(*route[0])
+
+        @pl.when(ok)
+        def _(index=index, target=target):
+            halo(index, target).start()
 
     for index, route in enumerate(routes):
         step_d, step_h = route[0]
@@ -200,59 +203,110 @@
             clear = 1.0 - covered
         return colour + [covered]
 
-    def send(view, hop):
-        peer = lax.rem(d + hop, groups)
+    odd = lax.rem(d, 2)
+    out_step = 2 * odd - 1
+    mate = d - out_step
+    pair = lax.div(d, 2)
+    beyond = odd * (groups - 1 - d) + (1 - odd) * d
+    handing = odd * (d - 1) + (1 - odd) * (groups - 2 - d)
+
+    def over(first, second, swap):
+        front = [jnp.where(swap, b, a) for a, b in zip(first, second)]
+        behind = [jnp.where(swap, a, b) for a, b in zip(first, second)]
+        clear = 1.0 - front[3]
+        return [f + clear * b for f, b in zip(front, behind)]
+
+    def load(ref, block, view):
+        return [ref[block, view, c] for c in range(4)]
+
+    def store(ref, block, view, image):
+        for c in range(4):
+            ref[block, view, c] = image[c]
+
+    def hand(view, block):
         return pltpu.make_async_remote_copy(
-            src_ref=outgoing.at[peer, view],
+            src_ref=outgoing.at[block, view],
+            dst_ref=handed.at[block, view],
+            send_sem=hand_send.at[view, block],
+            recv_sem=hand_recv.at[view, block],
+            device_id=(mate, h),
+            device_id_type=MESH,
+        )
+
+    def send(view, block):
+        return pltpu.make_async_remote_copy(
+            src_ref=outgoing.at[block, view],
             dst_ref=incoming.at[d, view],
-            send_sem=part_send.at[view, hop],
+            send_sem=part_send.at[view, block],
             recv_sem=part_recv.at[view, d],
-            device_id=(peer, h),
+            device_id=(block, h),
             device_id_type=MESH,
         )
 
-    for view in range(views):
-
-        def one_peer(hop, _):
-            peer = lax.rem(d + hop, groups)
-            image = partial(view, peer)
-            for c in range(4):
-                outgoing[peer, view, c] = image[c]
-            send(view, hop).start()
+    def receive(view, source):
+        return pltpu.make_async_remote_copy(
+            src_ref=outgoing.at[source, view],
+            dst_ref=incoming.at[source, view],
+            send_sem=part_send.at[view, source],
+            recv_sem=part_recv.at[view, source],
+            device_id=(source, h),
+            device_id_type=MESH,
+        )
+
+    def each(count, body):
+        def step(k, _):
+            body(k)
             return 0
 
-        lax.fori_loop(1, groups, one_peer, 0)
-
-    for view in range(views):
-        image = partial(view, d)
-        for c in range(4):
-            incoming[d, view, c] = image[c]
-
-    for view in range(views):
-
-        def arrived(hop, _):
-            source = lax.rem(d + hop, groups)
-            pltpu.make_async_remote_copy(
-                src_ref=outgoing.at[source, view],
-                dst_ref=incoming.at[source, view],
-                send_sem=part_send.at[view, hop],
-                recv_sem=part_recv.at[view, source],
-                device_id=(source, h),
-                device_id_type=MESH,
-            ).wait_recv()
-            return 0
-
-        lax.fori_loop(1, groups, arrived, 0)
+        lax.fori_loop(0, count, step, 0)
+
+    def hand_over(view, k):
+        block = d - out_step * (2 + k)
+        store(outgoing, block, view, partial(view, block))
+        hand(view, block).start()
+
+    def prepare(view, k):
+        block = d + out_step * (1 + k)
+        store(outgoing, block, view, partial(view, block))
+
+    def to_mate(view):
+        store(outgoing, mate, view, partial(view, mate))
+        send(view, mate).start()
+
+    def pass_on(view, k):
+        block = d + out_step * (1 + k)
+        hand(view, block).wait_recv()
+        own_part, other = load(outgoing, block, view), load(handed, block, view)
+        swap = reverse[view] != odd
+        store(outgoing, block, view, over(own_part, other, swap))
+        send(view, block).start()
+
+    each(views, lambda view: each(handing, lambda k: hand_over(view, k)))
+    each(views, to_mate)
+    each(views, lambda view: each(beyond, lambda k: prepare(view, k)))
+    each(views, lambda view: store(incoming, d, view, partial(view, d)))
+    each(views, lambda view: each(beyond, lambda k: pass_on(view, k)))
+
+    def finish(view):
         swap = reverse[view] == 1
-        total = [incoming[0, view, c] for c in range(4)]
-        for g in range(1, groups):
-            new = [incoming[g, view, c] for c in range(4)]
-            front = [jnp.where(swap, b, a) for a, b in zip(total, new)]
-            behind = [jnp.where(swap, a, b) for a, b in zip(total, new)]
-            clear = 1.0 - front[3]
-            total = [f + clear * b for f, b in zip(front, behind)]
+        receive(view, mate).wait_recv()
+        both = over(load(incoming, d, view), load(incoming, mate, view), reverse[view] != odd)
+        store(incoming, 2 * pair + 1, view, both)
+        sources = [jnp.where(j > pair, 2 * j, 2 * j + 1) for j in range(groups // 2)]
+        for j, source in enumerate(sources):
+
+            @pl.when(j != pair)
+            def _():
+                receive(view, source).wait_recv()
+
+        total = load(incoming, sources[0], view)
+        for source in sources[1:]:
+            total = over(total, load(incoming, source, view), swap)
         for c in range(4):
             out[c, view] = total[c]
+
+    for view in range(views):
+        finish(view)
 
     for index, route in enumerate(routes):
         ok, target = near(*route[0])
@@ -261,13 +315,12 @@
         def _(index=index, target=target):
             halo(index, target).wait_send()
 
-    for view in range(views):
-
-        def sent(hop, _):
-            send(view, hop).wait_send()
-            return 0
-
-        lax.fori_loop(1, groups, sent, 0)
+    def sent(view):
+        send(view, mate).wait_send()
+        each(handing, lambda k: hand(view, d - out_step * (2 + k)).wait_send())
+        each(beyond, lambda k: send(view, d + out_step * (1 + k)).wait_send())
+
+    each(views, sent)
 
 
 def on_device(groups, towers, density, light, gain, bias, shear, reverse):
@@ -287,9 +340,12 @@
             pltpu.VMEM((4, planes, rows + rows // 2, cols), jnp.float32),
             pltpu.VMEM((groups, views, 4, share, cols), jnp.float32),
             pltpu.VMEM((groups, views, 4, share, cols), jnp.float32),
+            pltpu.VMEM((groups, views, 4, share, cols), jnp.float32),
             pltpu.SemaphoreType.DMA,
             pltpu.SemaphoreType.DMA((6,)),
             pltpu.SemaphoreType.DMA((6,)),
+            pltpu.SemaphoreType.DMA((views, groups)),
+            pltpu.SemaphoreType.DMA((views, groups)),
             pltpu.SemaphoreType.DMA((views, groups)),
             pltpu.SemaphoreType.DMA((views, groups)),
         ],

time: 25.6 us -> 23.8 us (0.930)
  the two profiles are of different devices: /device:TPU:0 before, /device:TPU:1 now
where the time goes in v2:
time: 23.8 us; the launch traced here: 23.6 us
  Pallas kernels  22 us (92%)
  local copies, waits for them, and re-layouts  1.57 us (7%)
    pallas_call x1, Pallas kernels, on_device(): pl.pallas_call(functools.partial(kernel, groups, towers), name='render',...  22 us
    unnamed x1, local copies, waits for them, and re-layouts  1.57 us

profile of v2, /device:TPU:1, one launch (start us, length us, event | category | flops | bytes accessed | tf_op | source)
XLA Modules:
  0.0 23.6 jit_solution(121766882388578027)
XLA Ops:
  0.0 22.0 %render.1 = f32[4,4,16,128]{3,2,1,0:T(8,128)} custom-call(f32[8,64,128]{2,1,0:T(8,128)} %density.1, f32[3]{0:T(128)} %light.1, f32[3]{0:T(128)} %gain.1, f32[3]{0:T(128)} %bias.1, s32[4]{0:T(128)} %shear.1, s32[4]{0:T(128)} %reverse.1), custom_call_target="tpu_custom_call" | custom-call | tf_op jit(solution)/shard_map/render/pallas_call | solution.py:332
  22.0 1.6 %copy.8 = f32[4,4,16,128]{3,2,1,0:T(8,128)} copy(f32[4,4,16,128]{3,2,1,0:T(8,128)} %render.1) | data formatting | bytes 262144

commit v3 on v2

--- a/solution.py
+++ b/solution.py
@@ -64,12 +64,10 @@
         return ok, (d + step_d, h + step_h)
 
     barrier = pltpu.get_barrier_semaphore()
-    beside = [(0, 1), (0, -1), (1, 1), (1, -1), (-1, 1), (-1, -1)]
-    expected = jnp.int32(groups - 1)
-    for hop in range(1, groups):
-        pl.semaphore_signal(
-            barrier, inc=1, device_id=(lax.rem(d + hop, groups), h), device_id_type=MESH
-        )
+    beside = [(0, 1), (0, -1), (1, 1), (1, -1), (-1, 1), (-1, -1), (1, 0), (-1, 0)]
+    if groups > 4:
+        beside += [(step * hop, 0) for hop in range(2, groups) for step in (1, -1)]
+    expected = jnp.int32(0)
     for step_d, step_h in beside:
         ok, target = near(step_d, step_h)
         expected = expected + jnp.where(ok, 1, 0)
@@ -332,8 +330,8 @@
     return pl.pallas_call(
         functools.partial(kernel, groups, towers),
         name="render",
-        out_shape=jax.ShapeDtypeStruct((4, views, share, cols), jnp.float32),
-        in_specs=[pl.BlockSpec(memory_space=pl.ANY)] + [scalars] * 5,
+        out_shape=pltpu.VMEM((4, views, share, cols), jnp.float32),
+        in_specs=[pl.BlockSpec(memory_space=pltpu.HBM)] + [scalars] * 5,
         out_specs=pl.BlockSpec(memory_space=pltpu.VMEM),
         scratch_shapes=[
             pltpu.VMEM((planes + 2, tall + LEAD, cols), jnp.float32),
@@ -349,7 +347,7 @@
             pltpu.SemaphoreType.DMA((views, groups)),
             pltpu.SemaphoreType.DMA((views, groups)),
         ],
-        compiler_params=pltpu.CompilerParams(collective_id=0, has_side_effects=True),
+        compiler_params=pltpu.CompilerParams(collective_id=0, has_side_effects=True, vmem_limit_bytes=60 * 1024 * 1024),
     )(density, light, gain, bias, shear, reverse)
 
 

time: 23.8 us -> 22.2 us (0.933)
  local copies, waits for them, and re-layouts: 1.57 us -> 0.66 us
  Pallas kernels: 22 us -> 21.4 us
    unnamed x1, local copies, waits for them, and re-layouts: 1.57 us -> 0.66 us
    pallas_call x1, Pallas kernels: 22 us -> 21.4 us  [on_device(): pl.pallas_call(functools.partial(kernel, groups, towers), name='render',...]
where the time goes in v3:
time: 22.2 us; the launch traced here: 22.1 us
  Pallas kernels  21.4 us (96%)
  local copies, waits for them, and re-layouts  0.66 us (3%)
    pallas_call x1, Pallas kernels, on_device(): pl.pallas_call(functools.partial(kernel, groups, towers), name='render',...  21.4 us
    unnamed x1, local copies, waits for them, and re-layouts  0.66 us

profile of v3, /device:TPU:1, one launch (start us, length us, event | category | flops | bytes accessed | tf_op | source)
XLA Modules:
  0.0 22.1 jit_solution(12528431386728648901)
XLA Ops:
  0.0 21.4 %render.1 = f32[4,4,16,128]{3,2,1,0:T(8,128)S(1)} custom-call(f32[8,64,128]{2,1,0:T(8,128)} %density.1, f32[3]{0:T(128)} %light.1, f32[3]{0:T(128)} %gain.1, f32[3]{0:T(128)} %bias.1, s32[4]{0:T(128)} %shear.1, s32[4]{0:T(128)} %reverse.1), custom_call_target="tpu_custom_call" | custom-call | tf_op jit(solution)/shard_map/render/pallas_call | solution.py:330
  21.4 0.7 %copy.8 = f32[4,4,16,128]{3,2,1,0:T(8,128)} copy(f32[4,4,16,128]{3,2,1,0:T(8,128)S(1)} %render.1) | data formatting | bytes 262144

commit v4 on v3

--- a/solution.py
+++ b/solution.py
@@ -76,6 +76,39 @@
         def _(target=target):
             pl.semaphore_signal(barrier, inc=1, device_id=target, device_id_type=MESH)
 
+    pl.semaphore_wait(barrier, expected)
+
+    whole = pl.ds(0, planes)
+    inner = pl.ds(1, planes)
+    first, last = pl.ds(0, 1), pl.ds(planes - 1, 1)
+    low, high = pl.ds(0, 1), pl.ds(planes + 1, 1)
+    routes = [
+        ((0, -1), whole, (0, margin), inner, end),
+        ((1, -1), last, (0, margin), low, end),
+        ((-1, -1), first, (0, margin), high, end),
+        ((1, 0), last, (0, rows), low, LEAD),
+        ((-1, 0), first, (0, rows), high, LEAD),
+        ((0, 1), whole, (rows - LEAD, LEAD), inner, 0),
+    ]
+
+    def halo(index, reach):
+        step, from_planes, (row, count), to_planes, to_row = routes[index]
+        return pltpu.make_async_remote_copy(
+            src_ref=density.at[from_planes, pl.ds(row, count)],
+            dst_ref=volume.at[to_planes, pl.ds(to_row, count)],
+            send_sem=halo_send.at[index],
+            recv_sem=halo_recv.at[index],
+            device_id=reach,
+            device_id_type=MESH,
+        )
+
+    for index, route in enumerate(routes):
+        ok, target = near(*route[0])
+
+        @pl.when(ok)
+        def _(index=index, target=target):
+            halo(index, target).start()
+
     @pl.when(d == 0)
     def _():
         volume[0] = jnp.zeros(volume.shape[1:], jnp.float32)
@@ -129,39 +162,6 @@
         return 0
 
     lax.fori_loop(2, planes, early, 0)
-
-    pl.semaphore_wait(barrier, expected)
-
-    whole = pl.ds(0, planes)
-    inner = pl.ds(1, planes)
-    first, last = pl.ds(0, 1), pl.ds(planes - 1, 1)
-    low, high = pl.ds(0, 1), pl.ds(planes + 1, 1)
-    routes = [
-        ((0, -1), whole, (0, margin), inner, end),
-        ((1, -1), last, (0, margin), low, end),
-        ((-1, -1), first, (0, margin), high, end),
-        ((1, 0), last, (0, rows), low, LEAD),
-        ((-1, 0), first, (0, rows), high, LEAD),
-        ((0, 1), whole, (rows - LEAD, LEAD), inner, 0),
-    ]
-
-    def halo(index, reach):
-        step, from_planes, (row, count), to_planes, to_row = routes[index]
-        return pltpu.make_async_remote_copy(
-            src_ref=density.at[from_planes, pl.ds(row, count)],
-            dst_ref=volume.at[to_planes, pl.ds(to_row, count)],
-            send_sem=halo_send.at[index],
-            recv_sem=halo_recv.at[index],
-            device_id=reach,
-            device_id_type=MESH,
-        )
-
-    for index, route in enumerate(routes):
-        ok, target = near(*route[0])
-
-        @pl.when(ok)
-        def _(index=index, target=target):
-            halo(index, target).start()
 
     for index, route in enumerate(routes):
         step_d, step_h = route[0]
@@ -259,7 +259,7 @@
         lax.fori_loop(0, count, step, 0)
 
     def hand_over(view, k):
-        block = d - out_step * (2 + k)
+        block = odd * k + (1 - odd) * (groups - 1 - k)
         store(outgoing, block, view, partial(view, block))
         hand(view, block).start()
 
@@ -272,18 +272,18 @@
         send(view, mate).start()
 
     def pass_on(view, k):
-        block = d + out_step * (1 + k)
+        block = odd * (groups - 1 - k) + (1 - odd) * k
         hand(view, block).wait_recv()
         own_part, other = load(outgoing, block, view), load(handed, block, view)
         swap = reverse[view] != odd
         store(outgoing, block, view, over(own_part, other, swap))
         send(view, block).start()
 
-    each(views, lambda view: each(handing, lambda k: hand_over(view, k)))
+    each(handing, lambda k: each(views, lambda view: hand_over(view, k)))
     each(views, to_mate)
     each(views, lambda view: each(beyond, lambda k: prepare(view, k)))
     each(views, lambda view: store(incoming, d, view, partial(view, d)))
-    each(views, lambda view: each(beyond, lambda k: pass_on(view, k)))
+    each(beyond, lambda k: each(views, lambda view: pass_on(view, k)))
 
     def finish(view):
         swap = reverse[view] == 1

time: 22.2 us -> 20.7 us (0.932)
  the two profiles are of different devices: /device:TPU:1 before, /device:TPU:12 now
where the time goes in v4:
time: 20.7 us; the launch traced here: 20.5 us
  Pallas kernels  19.9 us (96%)
  local copies, waits for them, and re-layouts  0.66 us (3%)
    pallas_call x1, Pallas kernels, on_device(): pl.pallas_call(functools.partial(kernel, groups, towers), name='render',...  19.9 us
    unnamed x1, local copies, waits for them, and re-layouts  0.66 us

profile of v4, /device:TPU:12, one launch (start us, length us, event | category | flops | bytes accessed | tf_op | source)
XLA Modules:
  0.0 20.5 jit_solution(5903177295352988348)
XLA Ops:
  0.0 19.9 %render.1 = f32[4,4,16,128]{3,2,1,0:T(8,128)S(1)} custom-call(f32[8,64,128]{2,1,0:T(8,128)} %density.1, f32[3]{0:T(128)} %light.1, f32[3]{0:T(128)} %gain.1, f32[3]{0:T(128)} %bias.1, s32[4]{0:T(128)} %shear.1, s32[4]{0:T(128)} %reverse.1), custom_call_target="tpu_custom_call" | custom-call | tf_op jit(solution)/shard_map/render/pallas_call | solution.py:330
  19.9 0.7 %copy.8 = f32[4,4,16,128]{3,2,1,0:T(8,128)} copy(f32[4,4,16,128]{3,2,1,0:T(8,128)S(1)} %render.1) | data formatting | bytes 262144

commit v5 on v4

--- a/solution.py
+++ b/solution.py
@@ -163,25 +163,35 @@
 
     lax.fori_loop(2, planes, early, 0)
 
-    for index, route in enumerate(routes):
-        step_d, step_h = route[0]
+    def landed(index):
+        step_d, step_h = routes[index][0]
         ok, source = near(-step_d, -step_h)
 
         @pl.when(ok)
-        def _(index=index, source=source):
+        def _():
             halo(index, source).wait_recv()
 
-    def late(plane, _):
-        shade(plane, 0, LEAD, None)
-        shade(plane, rows - LEAD, LEAD, None)
-        for row, count in spans(rows, rows + margin, 16):
-            shade(plane, row, count, inside)
-        return 0
-
-    lax.fori_loop(1, planes + 1, late, 0)
-    for plane in (1, planes):
+    def shade_low():
+        for index in (3, 4, 5):
+            landed(index)
+        for plane in range(1, planes + 1):
+            shade(plane, 0, LEAD, None)
         for row, count in spans(LEAD, rows - LEAD, 16):
-            shade(plane, row, count, None)
+            for plane in (1, planes):
+                shade(plane, row, count, None)
+
+    def shade_high():
+        for index in (0, 1, 2):
+            landed(index)
+
+        def bottom(at, _):
+            for plane in (2 * at + 1, 2 * at + 2):
+                shade(plane, rows - LEAD, LEAD, None)
+                for row, count in spans(rows, rows + margin, 16):
+                    shade(plane, row, count, inside)
+            return 0
+
+        lax.fori_loop(0, planes // 2, bottom, 0)
 
     first_plane = d * planes
 
@@ -279,7 +289,23 @@
         store(outgoing, block, view, over(own_part, other, swap))
         send(view, block).start()
 
-    each(handing, lambda k: each(views, lambda view: hand_over(view, k)))
+    reach = lax.div((first_plane + planes - 1) * margin, jnp.int32(total_planes))
+
+    def hand_round(early):
+        def one(k):
+            block = odd * k + (1 - odd) * (groups - 1 - k)
+            ready = ((block + 1) * share + reach <= rows - LEAD) & (odd == 1)
+
+            @pl.when(ready if early else jnp.logical_not(ready))
+            def _():
+                each(views, lambda view: hand_over(view, k))
+
+        each(handing, one)
+
+    shade_low()
+    hand_round(True)
+    shade_high()
+    hand_round(False)
     each(views, to_mate)
     each(views, lambda view: each(beyond, lambda k: prepare(view, k)))
     each(views, lambda view: store(incoming, d, view, partial(view, d)))

time: 20.7 us -> 20 us (0.966)
  Pallas kernels: 19.9 us -> 19.2 us
    pallas_call x1, Pallas kernels: 19.9 us -> 19.2 us  [on_device(): pl.pallas_call(functools.partial(kernel, groups, towers), name='render',...]
where the time goes in v5:
time: 20 us; the launch traced here: 19.8 us
  Pallas kernels  19.2 us (96%)
  local copies, waits for them, and re-layouts  0.66 us (3%)
    pallas_call x1, Pallas kernels, on_device(): pl.pallas_call(functools.partial(kernel, groups, towers), name='render',...  19.2 us
    unnamed x1, local copies, waits for them, and re-layouts  0.66 us

profile of v5, /device:TPU:12, one launch (start us, length us, event | category | flops | bytes accessed | tf_op | source)
XLA Modules:
  0.0 19.8 jit_solution(4926891427513726493)
XLA Ops:
  0.0 19.2 %render.1 = f32[4,4,16,128]{3,2,1,0:T(8,128)S(1)} custom-call(f32[8,64,128]{2,1,0:T(8,128)} %density.1, f32[3]{0:T(128)} %light.1, f32[3]{0:T(128)} %gain.1, f32[3]{0:T(128)} %bias.1, s32[4]{0:T(128)} %shear.1, s32[4]{0:T(128)} %reverse.1), custom_call_target="tpu_custom_call" | custom-call | tf_op jit(solution)/shard_map/render/pallas_call | solution.py:356
  19.2 0.7 %copy.8 = f32[4,4,16,128]{3,2,1,0:T(8,128)} copy(f32[4,4,16,128]{3,2,1,0:T(8,128)S(1)} %render.1) | data formatting | bytes 262144

commit v6 on v5

--- a/solution.py
+++ b/solution.py
@@ -83,12 +83,12 @@
     first, last = pl.ds(0, 1), pl.ds(planes - 1, 1)
     low, high = pl.ds(0, 1), pl.ds(planes + 1, 1)
     routes = [
+        ((1, 0), last, (0, rows), low, LEAD),
+        ((-1, 0), first, (0, rows), high, LEAD),
+        ((0, 1), whole, (rows - LEAD, LEAD), inner, 0),
         ((0, -1), whole, (0, margin), inner, end),
         ((1, -1), last, (0, margin), low, end),
         ((-1, -1), first, (0, margin), high, end),
-        ((1, 0), last, (0, rows), low, LEAD),
-        ((-1, 0), first, (0, rows), high, LEAD),
-        ((0, 1), whole, (rows - LEAD, LEAD), inner, 0),
     ]
 
     def halo(index, reach):
@@ -172,7 +172,7 @@
             halo(index, source).wait_recv()
 
     def shade_low():
-        for index in (3, 4, 5):
+        for index in (0, 1, 2):
             landed(index)
         for plane in range(1, planes + 1):
             shade(plane, 0, LEAD, None)
@@ -181,7 +181,7 @@
                 shade(plane, row, count, None)
 
     def shade_high():
-        for index in (0, 1, 2):
+        for index in (3, 4, 5):
             landed(index)
 
         def bottom(at, _):

time: 20 us -> 19.6 us (0.980)
  Pallas kernels: 19.2 us -> 18.8 us
    pallas_call x1, Pallas kernels: 19.2 us -> 18.8 us  [on_device(): pl.pallas_call(functools.partial(kernel, groups, towers), name='render',...]
where the time goes in v6:
time: 19.6 us; the launch traced here: 19.5 us
  Pallas kernels  18.8 us (96%)
  local copies, waits for them, and re-layouts  0.66 us (3%)
    pallas_call x1, Pallas kernels, on_device(): pl.pallas_call(functools.partial(kernel, groups, towers), name='render',...  18.8 us
    unnamed x1, local copies, waits for them, and re-layouts  0.66 us

profile of v6, /device:TPU:12, one launch (start us, length us, event | category | flops | bytes accessed | tf_op | source)
XLA Modules:
  0.0 19.5 jit_solution(15474568533597259923)
XLA Ops:
  0.0 18.8 %render.1 = f32[4,4,16,128]{3,2,1,0:T(8,128)S(1)} custom-call(f32[8,64,128]{2,1,0:T(8,128)} %density.1, f32[3]{0:T(128)} %light.1, f32[3]{0:T(128)} %gain.1, f32[3]{0:T(128)} %bias.1, s32[4]{0:T(128)} %shear.1, s32[4]{0:T(128)} %reverse.1), custom_call_target="tpu_custom_call" | custom-call | tf_op jit(solution)/shard_map/render/pallas_call | solution.py:356
  18.8 0.7 %copy.8 = f32[4,4,16,128]{3,2,1,0:T(8,128)} copy(f32[4,4,16,128]{3,2,1,0:T(8,128)S(1)} %render.1) | data formatting | bytes 262144
